TPU v7x, 512 devices: a whole 4x4x16 slice. The times are simulated.
512 devices in a mesh: sample: 32 (over y, x, core), space: 16 (over z).
Axes of the slice: x: 4, y: 4, z: 16, core: 2. Of those that a mesh axis runs over, the one named last changes fastest.
Arguments:
- volumes: bfloat16 [32, 32, 64, 16, 128], P('sample', None, 'space'), may hold values from -360 to 360
- depth_kernel: float32 [32, 27], replicated, may hold values from -1.25 to 1.25
- point_weight: bfloat16 [32, 32], replicated, may hold values from -1 to 1
- cotangent: bfloat16 [32, 32, 64, 16, 128], P('sample', None, 'space'), may hold values from -4.1 to 4.1
Outputs:
- whitened: bfloat16 [32, 32, 64, 16, 128], P('sample', None, 'space')
- d_volumes: bfloat16 [32, 32, 64, 16, 128], P('sample', None, 'space')
- d_point: float32 [32, 32], replicated
- d_kernel: float32 [32, 27], replicated
All inputs are finite; a program needn't handle non-finite values.
Results may differ from a plain program's by a relative error of at most 0.0067.
Values may be sent and summed in bfloat16 or wider, within the bound.
No kernel may reach another device: no remote copies, remote signals or barrier semaphores. Data moves between devices by JAX's collectives and lax.ppermute only.
A program may use at most 64 MiB of HBM per device.

v0:
```python
from functools import partial
import math
import jax
import jax.numpy as jnp
from jax import lax
from jax.sharding import PartitionSpec as P

GSIZE = 16
NEWTON = 5
GROUPS = 2
epsilon = 1e-05
highest = lax.Precision.HIGHEST


def with_halo(block, sides, width):
    for axis, dim in sides:
        count = lax.axis_size(axis)
        forward = [(i, i + 1) for i in range(count - 1)]
        backward = [(target, source) for source, target in forward]
        low = lax.ppermute(
            lax.slice_in_dim(block, block.shape[dim] - width, None, axis=dim), axis, forward
        )
        high = lax.ppermute(lax.slice_in_dim(block, 0, width, axis=dim), axis, backward)
        block = jnp.concatenate([low, block, high], axis=dim)
    return block


def matmul_high(matrix, operand):
    return jnp.matmul(matrix, operand, precision=highest)


def contract_rows(matrix, operand):
    return jnp.einsum(
        "cv,dv->cd", matrix, operand, precision=highest, preferred_element_type=jnp.float32
    )


def contract_cols(matrix, operand):
    return jnp.einsum(
        "kc,kv->cv", matrix, operand, precision=highest, preferred_element_type=jnp.float32
    )


def block_diagonal(blocks):
    identity = jnp.eye(blocks.shape[0], dtype=blocks.dtype)
    full_size = blocks.shape[0] * blocks.shape[1]
    return jnp.einsum("gh,gij->gihj", identity, blocks, precision=highest).reshape(
        full_size, full_size
    )


def whiten_stats(first_sums, second_sums, voxel_count):
    groups = second_sums.shape[0]
    group_size = second_sums.shape[1]
    average = (first_sums / voxel_count).reshape(groups, group_size)
    identity = jnp.eye(group_size, dtype=second_sums.dtype)
    covariance = (
        second_sums / voxel_count - average[:, :, None] * average[:, None, :] + epsilon * identity
    )
    traces = jnp.trace(covariance, axis1=1, axis2=2)
    normed = covariance / traces[:, None, None]
    project = jnp.broadcast_to(identity, covariance.shape)
    for newton_step in range(NEWTON):
        cubed = matmul_high(matmul_high(project, project), project)
        project = 0.5 * (3.0 * project - matmul_high(cubed, normed))
    whiten_mat = project / jnp.sqrt(traces)[:, None, None]
    offset = jnp.einsum("gij,gj->gi", whiten_mat, average, precision=highest)
    return (whiten_mat, offset)


def adjoint_terms(pull_back, whiten_mat, grad_first, grad_second):
    d_first, d_second = pull_back(
        (grad_second, -grad_first.reshape(whiten_mat.shape[0], whiten_mat.shape[1]))
    )
    adjoint = block_diagonal(jnp.swapaxes(whiten_mat, 1, 2))
    symmetric = block_diagonal(d_second + jnp.swapaxes(d_second, 1, 2))
    return (d_first, adjoint, symmetric)


def gradient_signal(adjoint, d_first, symmetric, grad_part, mixed_part):
    first_term = jnp.dot(adjoint, grad_part, precision=highest, preferred_element_type=jnp.float32)
    third_term = jnp.dot(
        symmetric, mixed_part, precision=highest, preferred_element_type=jnp.float32
    )
    return first_term + d_first[:, None] + third_term


def pad_sides(extended):
    return jnp.pad(extended, ((0, 0), (0, 0), (1, 1), (1, 1)))


def tap_cells(padded, tap_index, depth_cells):
    plane_off = tap_index // 9
    row_off = tap_index // 3 % 3
    col_off = tap_index % 3
    height = padded.shape[2] - 2
    width_cells = padded.shape[3] - 2
    return padded[
        :,
        plane_off : plane_off + depth_cells,
        row_off : row_off + height,
        col_off : col_off + width_cells,
    ]


def depth_conv(extended, kernel, depth_cells):
    padded = pad_sides(extended)
    summed = jnp.zeros(
        (extended.shape[0], depth_cells, extended.shape[2], extended.shape[3]), jnp.float32
    )
    for tap_index in range(27):
        summed = summed + kernel[:, tap_index][:, None, None, None] * tap_cells(
            padded, tap_index, depth_cells
        ).astype(jnp.float32)
    return summed


def depth_adjoint(grad_ext, kernel, depth_cells):
    padded = pad_sides(grad_ext)
    height = grad_ext.shape[2]
    width_cells = grad_ext.shape[3]
    summed = jnp.zeros((grad_ext.shape[0], depth_cells, height, width_cells), jnp.float32)
    for tap_index in range(27):
        plane_off = 2 - tap_index // 9
        row_off = 2 - tap_index // 3 % 3
        col_off = 2 - tap_index % 3
        summed = (
            summed
            + kernel[:, tap_index][:, None, None, None]
            * padded[
                :,
                plane_off : plane_off + depth_cells,
                row_off : row_off + height,
                col_off : col_off + width_cells,
            ]
        )
    return summed


def on_device(volumes, depth_kernel, point_weight, cotangent):
    volume = volumes[0]
    grad_in = cotangent[0]
    channels, depth_cells, height, width_cells = volume.shape
    voxels = depth_cells * height * width_cells
    voxel_count = float(voxels * lax.axis_size("sample") * lax.axis_size("space"))
    grad_flat = grad_in.reshape(channels, voxels)
    extended = with_halo(volume, (("space", 1),), 1)
    hidden = (
        depth_conv(extended, depth_kernel, depth_cells)
        .astype(jnp.bfloat16)
        .reshape(channels, voxels)
    )
    mixed_out = jnp.dot(point_weight, hidden, preferred_element_type=jnp.float32).astype(
        jnp.bfloat16
    )
    grouped = mixed_out.reshape(GROUPS, GSIZE, voxels)
    local_first = jnp.sum(mixed_out.astype(jnp.float32), axis=1)
    local_second = jnp.einsum("giv,gjv->gij", grouped, grouped, preferred_element_type=jnp.float32)
    grad_first = jnp.sum(grad_flat.astype(jnp.float32), axis=1)
    grad_second = jnp.einsum(
        "giv,gjv->gij",
        grad_flat.reshape(GROUPS, GSIZE, voxels),
        grouped,
        preferred_element_type=jnp.float32,
    )
    padded_x = pad_sides(extended)
    weight_f = point_weight.astype(jnp.float32)
    stats_fn = partial(whiten_stats, voxel_count=voxel_count)
    first_sums, second_sums, grad_first, grad_second = lax.psum(
        (local_first, local_second, grad_first, grad_second), ("sample", "space")
    )
    (whiten_mat, offset), pull_back = jax.vjp(stats_fn, first_sums, second_sums)
    d_first, adjoint, symmetric = adjoint_terms(pull_back, whiten_mat, grad_first, grad_second)
    whitened = (
        jnp.dot(
            block_diagonal(whiten_mat),
            mixed_out,
            precision=highest,
            preferred_element_type=jnp.float32,
        )
        - offset.reshape(channels)[:, None]
    ).astype(jnp.bfloat16)
    d_mixed = gradient_signal(adjoint, d_first, symmetric, grad_flat, mixed_out)
    d_hidden = contract_cols(weight_f, d_mixed).reshape(channels, depth_cells, height, width_cells)
    grad_ext = with_halo(d_hidden, (("space", 1),), 1)
    kernel_terms = jnp.stack(
        [
            jnp.sum(
                d_hidden * tap_cells(padded_x, tap_index, depth_cells).astype(jnp.float32),
                axis=(1, 2, 3),
            )
            for tap_index in range(27)
        ],
        axis=1,
    )
    d_point, d_kernel = lax.psum(
        (contract_rows(d_mixed, hidden), kernel_terms), ("sample", "space")
    )
    d_volume = depth_adjoint(grad_ext, depth_kernel, depth_cells).astype(jnp.bfloat16)
    scale_out = 1.0 / math.sqrt(voxel_count)
    return (
        whitened.reshape(1, channels, depth_cells, height, width_cells),
        d_volume[None],
        d_point * scale_out,
        d_kernel * scale_out,
    )


def solution(mesh):
    in_specs = (
        P("sample", None, "space", None, None),
        P(),
        P(),
        P("sample", None, "space", None, None),
    )
    out_specs = (
        P("sample", None, "space", None, None),
        P("sample", None, "space", None, None),
        P(),
        P(),
    )
    return jax.shard_map(
        on_device, mesh=mesh, in_specs=in_specs, out_specs=out_specs, check_vma=False
    )
```

profile of v0, /device:TPU:1, one launch (start us, length us, event | category | flops | bytes accessed | tf_op | source)
XLA Modules:
  0.0 388.2 jit_solution(1286581559153312555)
XLA Ops:
  1.8 4.4 %collective-permute-start = (bf16[32,1,16,128]{3,2,1,0:T(8,128)(2,1)S(1)}, bf16[32,1,16,128]{3,2,1,0:T(8,128)(2,1)S(1)}, u32[]{:S(2)}, u32[]{:S(2)}) collective-permute-start(bf16[32,1,16,128]{3,2,1,0:T(8,128)(2,1)S(1)} %get-tuple-element.77), channel_id=1, source_target_pairs={{0,1},{1,2},{2,3},{3,4},{4,5},{5,6},{6,7},{7,8},{8,9},{9,10},{10,1... | collective-permute-start | bytes 393224 | tf_op jit(solution)/shard_map/ppermute | solution.py:20
  9.2 1.9 slice_reduce_fusion.25
  11.1 2.6 slice_reduce_fusion.26
  13.7 2.1 reshape_squeeze.3
  15.8 2.1 reshape_reshape_squeeze.3
  17.8 2.2 reshape.120
  22.5 3.0 select_maximum_fusion.2
  25.5 7.8 %fusion.59 = bf16[32,4,16,128]{3,2,1,0:T(8,128)(2,1)S(1)} fusion(bf16[32,4,16,128]{3,2,1,0:T(8,128)(2,1)S(1)} %bitcast.174, bf16[32,1,16,128]{3,2,1,0:T(8,128)(2,1)} %collective-permute-done.1, bf16[32,1,16,128]{3,2,1,0:T(8,128)(2,1)S(1)} %collective-permute-done, f32[32]{0:T(128)} %get-tuple-element.67, f32[32]{0:T(128)} %get-tuple-element.68, ...), kind=kLoop, calls=%fused_computation.140 | loop fusion | flops 21757952 | bytes 13897088 | tf_op jit(solution)/shard_map/convert_element_type | solution.py:150
  36.4 111.9 %all-reduce.3 = (f32[32]{0:T(128)}, f32[2,16,16]{2,1,0:T(8,128)}, f32[2,16,16]{1,2,0:T(8,128)}, f32[32]{0:T(128)}) all-reduce(f32[32]{0:T(128)} %get-tuple-element.91, f32[2,16,16]{2,1,0:T(8,128)} %fusion.215, f32[2,16,16]{1,2,0:T(8,128)} %convolution_bitcast_fusion, ...), channel_id=1, replica_groups=mesh['sample'=32,'space'=16] {'sample','space'}, use_global_device_ids=true, to_apply=%region_2.3 | all-reduce | flops 1088 | bytes 8704 | tf_op jit(solution)/shard_map/psum | solution.py:169
  162.7 1.6 fusion.212
  168.7 1.5 fusion.211
  174.2 1.5 fusion.210
  179.6 1.5 fusion.209
  198.2 1.6 fusion.208
  205.4 1.6 multiply_reduce_fusion.2
  209.7 1.5 multiply_reduce_fusion.3
  214.2 1.4 multiply_reduce_fusion.1
  218.5 1.5 multiply_bitcast_fusion
  220.0 1.4 reshape.118
  221.4 1.4 reshape.117
  222.9 1.7 convolution_add_fusion.1
  225.9 1.5 fusion.91
  228.9 6.7 %fusion.60 = (f32[32]{0:T(128)S(1)}, f32[32]{0:T(128)S(1)}, f32[32]{0:T(128)}, f32[32]{0:T(128)}, f32[32]{0:T(128)}, /*index=5*/f32[32]{0:T(128)}, f32[32]{0:T(1...) fusion(f32[32,4,16,128]{3,2,1,0:T(8,128)S(1)} %bitcast.164, ...), kind=kLoop, calls=%fused_computation.141 | loop fusion | flops 14155200 | bytes 10488064 | tf_op jit(solution)/shard_map/reduce_sum | solution.py:188
  238.4 1.4 reshape.115
  239.8 4.3 %fusion.57 = (f32[32]{0:T(128)}, f32[32]{0:T(128)}, f32[32]{0:T(128)}, f32[32]{0:T(128)}, f32[32]{0:T(128)}, /*index=5*/f32[32]{0:T(128)}, f32[32]{0:T(128)}, f32[32]{0:T(128)}) fusion(f32[32,4,16,128]{3,2,1,0:T(8,128)S(1)} %bitcast.166, bf16[32,6,18,130]{3,2,1,0:T(8,128)(2,1)S(1)} %select_maximum_fusion.2, bf16[32,4,16,128]{3,2,1,0:T(8,128)(2,1)} %bitcast.172, ...), kind=kLoop, calls=%fused_computation.138 | loop fusion | flops 6815488 | bytes 4981760 | tf_op jit(solution)/shard_map/reduce_sum | solution.py:188
  244.4 2.8 stack.111
  247.2 99.9 %all-reduce.2 = (f32[32,32]{1,0:T(8,128)S(1)}, f32[32,27]{0,1:T(8,128)S(1)}) all-reduce(f32[32,32]{1,0:T(8,128)} %fusion.91, f32[32,27]{0,1:T(8,128)S(1)} %stack.111), channel_id=1, replica_groups=mesh['sample'=32,'space'=16] {'sample','space'}, use_global_device_ids=true, to_apply=%region_11.12 | all-reduce | flops 1888 | bytes 15104 | tf_op jit(solution)/shard_map/psum | solution.py:196
  347.1 3.3 collective-permute-start.2
  351.6 1.6 fusion.5
  355.6 3.7 collective-permute-done.3
  359.3 3.4 select_maximum_fusion
  363.0 25.1 %fusion.94 = bf16[1,32,4,16,128]{4,3,2,1,0:T(8,128)(2,1)} fusion(f32[32,6,18,130]{3,2,1,0:T(8,128)} %select_maximum_fusion, f32[32]{0:T(128)S(1)} %copy-done.23, f32[32]{0:T(128)S(1)} %copy-done.24, f32[32]{0:T(128)S(1)} %copy-done.26, f32[32]{0:T(128)S(1)} %copy-done.27, f32[32,4,16,128]{3,2,1,0:T(8,128)S(1)} %bitcast.168, ...), kind=kLoop, calls=%fused_computation.206 | loop fusion | flops 14680064 | bytes 27266432 | tf_op jit(solution)/shard_map/broadcast_in_dim | solution.py:203
  (180 shorter events, 76.9 us)
Async XLA Ops:
  1.8 20.8 %collective-permute-start = (bf16[32,1,16,128]{3,2,1,0:T(8,128)(2,1)S(1)}, bf16[32,1,16,128]{3,2,1,0:T(8,128)(2,1)S(1)}, u32[]{:S(2)}, u32[]{:S(2)}) collective-permute-start(bf16[32,1,16,128]{3,2,1,0:T(8,128)(2,1)S(1)} %get-tuple-element.77), channel_id=1, source_target_pairs={{0,1},{1,2},{2,3},{3,4},{4,5},{5,6},{6,7},{7,8},{8,9},{9,10},{10,1... | collective-permute-start | bytes 393224 | tf_op jit(solution)/shard_map/ppermute | solution.py:20
  6.1 16.4 %collective-permute-start.1 = (bf16[32,1,16,128]{3,2,1,0:T(8,128)(2,1)S(1)}, bf16[32,1,16,128]{3,2,1,0:T(8,128)(2,1)}, u32[]{:S(2)}, u32[]{:S(2)}) collective-permute-start(bf16[32,1,16,128]{3,2,1,0:T(8,128)(2,1)S(1)} %get-tuple-element.78), channel_id=1, source_target_pairs={{1,0},{2,1},{3,2},{4,3},{5,4},{6,5},{7,6},{8,7},{9,8},{10,9},{11,1... | collective-permute-start | bytes 393224 | tf_op jit(solution)/shard_map/ppermute | solution.py:23
  34.5 191.4 %copy-start.1 = (bf16[8192,32]{0,1:T(8,128)(2,1)}, bf16[8192,32]{0,1:T(8,128)(2,1)S(1)}, u32[]{:S(2)}) copy-start(bf16[8192,32]{0,1:T(8,128)(2,1)S(1)} %get-tuple-element.92) | copy-start | bytes 1572868
  244.2 118.6 %copy-start.17 = (f32[32]{0:T(128)S(1)}, f32[32]{0:T(128)}, u32[]{:S(2)}) copy-start(f32[32]{0:T(128)} %get-tuple-element.61) | copy-start | bytes 388
  244.2 118.6 %copy-start.18 = (f32[32]{0:T(128)S(1)}, f32[32]{0:T(128)}, u32[]{:S(2)}) copy-start(f32[32]{0:T(128)} %get-tuple-element.62) | copy-start | bytes 388
  244.2 118.6 %copy-start.19 = (f32[32]{0:T(128)S(1)}, f32[32]{0:T(128)}, u32[]{:S(2)}) copy-start(f32[32]{0:T(128)} %get-tuple-element.63) | copy-start | bytes 388
  244.2 118.6 %copy-start.20 = (f32[32]{0:T(128)S(1)}, f32[32]{0:T(128)}, u32[]{:S(2)}) copy-start(f32[32]{0:T(128)} %get-tuple-element.64) | copy-start | bytes 388
  244.2 118.6 %copy-start.21 = (f32[32]{0:T(128)S(1)}, f32[32]{0:T(128)}, u32[]{:S(2)}) copy-start(f32[32]{0:T(128)} %get-tuple-element.65) | copy-start | bytes 388
  244.2 118.6 %copy-start.22 = (f32[32]{0:T(128)S(1)}, f32[32]{0:T(128)}, u32[]{:S(2)}) copy-start(f32[32]{0:T(128)} %get-tuple-element.66) | copy-start | bytes 388
  244.2 118.6 %copy-start.23 = (f32[32]{0:T(128)S(1)}, f32[32]{0:T(128)}, u32[]{:S(2)}) copy-start(f32[32]{0:T(128)} %get-tuple-element.67) | copy-start | bytes 388
  244.2 118.6 %copy-start.24 = (f32[32]{0:T(128)S(1)}, f32[32]{0:T(128)}, u32[]{:S(2)}) copy-start(f32[32]{0:T(128)} %get-tuple-element.68) | copy-start | bytes 388
  244.2 118.6 %copy-start.25 = (f32[32]{0:T(128)S(1)}, f32[32]{0:T(128)}, u32[]{:S(2)}) copy-start(f32[32]{0:T(128)} %get-tuple-element.42) | copy-start | bytes 388
  244.2 118.6 %copy-start.26 = (f32[32]{0:T(128)S(1)}, f32[32]{0:T(128)}, u32[]{:S(2)}) copy-start(f32[32]{0:T(128)} %get-tuple-element.43) | copy-start | bytes 388
  244.2 118.6 %copy-start.27 = (f32[32]{0:T(128)S(1)}, f32[32]{0:T(128)}, u32[]{:S(2)}) copy-start(f32[32]{0:T(128)} %get-tuple-element.44) | copy-start | bytes 388
  244.2 118.6 %copy-start.28 = (f32[32]{0:T(128)S(1)}, f32[32]{0:T(128)}, u32[]{:S(2)}) copy-start(f32[32]{0:T(128)} %get-tuple-element.45) | copy-start | bytes 388
  244.3 118.6 %copy-start.29 = (f32[32]{0:T(128)S(1)}, f32[32]{0:T(128)}, u32[]{:S(2)}) copy-start(f32[32]{0:T(128)} %get-tuple-element.46) | copy-start | bytes 388
  244.3 118.6 %copy-start.30 = (f32[32]{0:T(128)S(1)}, f32[32]{0:T(128)}, u32[]{:S(2)}) copy-start(f32[32]{0:T(128)} %get-tuple-element.47) | copy-start | bytes 388
  244.3 118.6 %copy-start.31 = (f32[32]{0:T(128)S(1)}, f32[32]{0:T(128)}, u32[]{:S(2)}) copy-start(f32[32]{0:T(128)} %get-tuple-element.48) | copy-start | bytes 388
  244.3 118.6 %copy-start.32 = (f32[32]{0:T(128)S(1)}, f32[32]{0:T(128)}, u32[]{:S(2)}) copy-start(f32[32]{0:T(128)} %get-tuple-element.49) | copy-start | bytes 388
  244.3 118.6 %copy-start.33 = (f32[32]{0:T(128)S(1)}, f32[32]{0:T(128)}, u32[]{:S(2)}) copy-start(f32[32]{0:T(128)} %get-tuple-element.50) | copy-start | bytes 388
  244.3 118.6 %copy-start.34 = (f32[32]{0:T(128)S(1)}, f32[32]{0:T(128)}, u32[]{:S(2)}) copy-start(f32[32]{0:T(128)} %get-tuple-element.51) | copy-start | bytes 388
  244.3 118.6 %copy-start.35 = (f32[32]{0:T(128)S(1)}, f32[32]{0:T(128)}, u32[]{:S(2)}) copy-start(f32[32]{0:T(128)} %get-tuple-element.52) | copy-start | bytes 388
  244.3 118.6 %copy-start.36 = (f32[32]{0:T(128)S(1)}, f32[32]{0:T(128)}, u32[]{:S(2)}) copy-start(f32[32]{0:T(128)} %get-tuple-element.53) | copy-start | bytes 388
  244.3 118.6 %copy-start.37 = (f32[32]{0:T(128)S(1)}, f32[32]{0:T(128)}, u32[]{:S(2)}) copy-start(f32[32]{0:T(128)} %get-tuple-element.54) | copy-start | bytes 388
  244.3 118.6 %copy-start.38 = (f32[32]{0:T(128)S(1)}, f32[32]{0:T(128)}, u32[]{:S(2)}) copy-start(f32[32]{0:T(128)} %get-tuple-element.55) | copy-start | bytes 388
  244.4 118.6 %copy-start.39 = (f32[32]{0:T(128)S(1)}, f32[32]{0:T(128)}, u32[]{:S(2)}) copy-start(f32[32]{0:T(128)} %get-tuple-element.56) | copy-start | bytes 388
  244.4 118.6 %copy-start.40 = (f32[32]{0:T(128)S(1)}, f32[32]{0:T(128)}, u32[]{:S(2)}) copy-start(f32[32]{0:T(128)} %get-tuple-element.57) | copy-start | bytes 388
  244.4 118.6 %copy-start.41 = (f32[32]{0:T(128)S(1)}, f32[32]{0:T(128)}, u32[]{:S(2)}) copy-start(f32[32]{0:T(128)} %get-tuple-element.58) | copy-start | bytes 388
  244.4 118.6 %copy-start.42 = (f32[32]{0:T(128)S(1)}, f32[32]{0:T(128)}, u32[]{:S(2)}) copy-start(f32[32]{0:T(128)} %get-tuple-element.59) | copy-start | bytes 388
  244.4 118.6 %copy-start.43 = (f32[32]{0:T(128)S(1)}, f32[32]{0:T(128)}, u32[]{:S(2)}) copy-start(f32[32]{0:T(128)} %get-tuple-element.60) | copy-start | bytes 388
  347.1 8.5 %collective-permute-start.2 = (f32[32,1,16,128]{3,2,1,0:T(8,128)}, f32[32,1,16,128]{3,2,1,0:T(8,128)S(1)}, u32[]{:S(2)}, u32[]{:S(2)}) collective-permute-start(f32[32,1,16,128]{3,2,1,0:T(8,128)} %get-tuple-element.75), channel_id=1, source_target_pairs={{0,1},{1,2},{2,3},{3,4},{4,5},{5,6},{6,7},{7,8},{8,9},{9,10},{10,1... | collective-permute-start | bytes 786440 | tf_op jit(solution)/shard_map/ppermute | solution.py:20
  350.3 9.0 %collective-permute-start.3 = (f32[32,1,16,128]{3,2,1,0:T(8,128)}, f32[32,1,16,128]{3,2,1,0:T(8,128)S(1)}, u32[]{:S(2)}, u32[]{:S(2)}) collective-permute-start(f32[32,1,16,128]{3,2,1,0:T(8,128)} %get-tuple-element.76), channel_id=1, source_target_pairs={{1,0},{2,1},{3,2},{4,3},{5,4},{6,5},{7,6},{8,7},{9,8},{10,9},{11,1... | collective-permute-start | bytes 786440 | tf_op jit(solution)/shard_map/ppermute | solution.py:23
  (17 other events, 113.1 us)
where the time goes:
time: 394 us; the launch traced here: 388 us
  blocking collectives  212 us (54%)
  other arithmetic  67.2 us (17%)
  local copies, waits for them, and re-layouts  48.5 us (12%)
  matrix products  45.2 us (11%)
  starting transfers between devices  10.2 us (3%)
    psum x1, blocking collectives, on_device(): lax.psum((local_first, local_second, grad_first, grad_second), ('sample',...  112 us
    psum x1, blocking collectives, on_device(): lax.psum((contract_rows(d_mixed, hidden), kernel_terms), ('sample', 'spac...  99.9 us
    dot_general x40, matrix products, matmul_high(): return jnp.matmul(matrix, operand, precision=highest)  33.2 us
    broadcast_in_dim x1, other arithmetic, on_device(): d_volume[None]  25.1 us
    reduce_sum x2, other arithmetic, on_device(): jnp.sum(d_hidden * tap_cells(padded_x, tap_index, depth_cells).astype(jnp...  11 us
  transfers between devices with their start and end apart: 4, of which 2 were waited for; matrix products, arithmetic and copies ran while one was open for 5% of the time, Pallas kernels for 0%

commit v1 on v0

--- a/solution.py
+++ b/solution.py
@@ -194,7 +194,7 @@
         axis=1,
     )
     d_point, d_kernel = lax.psum(
-        (contract_rows(d_mixed, hidden), kernel_terms), ("sample", "space")
+        lax.psum((contract_rows(d_mixed, hidden), kernel_terms), "sample"), "space"
     )
     d_volume = depth_adjoint(grad_ext, depth_kernel, depth_cells).astype(jnp.bfloat16)
     scale_out = 1.0 / math.sqrt(voxel_count)

time: 394 us -> 470 us (1.19)
  the two profiles are of different devices: /device:TPU:1 before, /device:TPU:96 now
where the time goes in v1:
time: 470 us; the launch traced here: 464 us
  blocking collectives  283 us (60%)
  other arithmetic  67.2 us (14%)
  local copies, waits for them, and re-layouts  48.5 us (10%)
  matrix products  45.2 us (10%)
  starting transfers between devices  14.3 us (3%)
    psum x1, blocking collectives, on_device(): lax.psum((contract_rows(d_mixed, hidden), kernel_terms), 'sample')  124 us
    psum x1, blocking collectives, on_device(): lax.psum((local_first, local_second, grad_first, grad_second), ('sample',...  107 us
    psum x1, blocking collectives, on_device(): lax.psum(lax.psum((contract_rows(d_mixed, hidden), kernel_terms), 'sample...  52.4 us
    dot_general x40, matrix products, matmul_high(): return jnp.matmul(matrix, operand, precision=highest)  33.2 us
    broadcast_in_dim x1, other arithmetic, on_device(): d_volume[None]  25.1 us
    reduce_sum x2, other arithmetic, on_device(): jnp.sum(d_hidden * tap_cells(padded_x, tap_index, depth_cells).astype(jnp...  11 us
    ppermute x2, starting transfers between devices, with_halo(): lax.ppermute(lax.slice_in_dim(block, block.shape[dim] - width, None, axis...  10.4 us
  transfers between devices with their start and end apart: 4, of which 1 were waited for; matrix products, arithmetic and copies ran while one was open for 4% of the time, Pallas kernels for 0%

profile of v1, /device:TPU:96, one launch (start us, length us, event | category | flops | bytes accessed | tf_op | source)
XLA Modules:
  0.0 464.0 jit_solution(16114698769366652999)
XLA Ops:
  1.8 5.0 %collective-permute-start = (bf16[32,1,16,128]{3,2,1,0:T(8,128)(2,1)S(1)}, bf16[32,1,16,128]{3,2,1,0:T(8,128)(2,1)S(1)}, u32[]{:S(2)}, u32[]{:S(2)}) collective-permute-start(bf16[32,1,16,128]{3,2,1,0:T(8,128)(2,1)S(1)} %get-tuple-element.79), channel_id=1, source_target_pairs={{0,1},{1,2},{2,3},{3,4},{4,5},{5,6},{6,7},{7,8},{8,9},{9,10},{10,1... | collective-permute-start | bytes 393224 | tf_op jit(solution)/shard_map/ppermute | solution.py:20
  6.8 1.9 collective-permute-start.1
  10.5 1.9 slice_reduce_fusion.25
  12.4 2.6 slice_reduce_fusion.26
  15.0 2.1 reshape_squeeze.3
  17.1 2.1 reshape_reshape_squeeze.3
  19.1 2.2 reshape.120
  23.8 3.0 select_maximum_fusion.2
  26.8 7.8 %fusion.59 = bf16[32,4,16,128]{3,2,1,0:T(8,128)(2,1)S(1)} fusion(bf16[32,4,16,128]{3,2,1,0:T(8,128)(2,1)S(1)} %bitcast.174, bf16[32,1,16,128]{3,2,1,0:T(8,128)(2,1)} %collective-permute-done.1, bf16[32,1,16,128]{3,2,1,0:T(8,128)(2,1)S(1)} %collective-permute-done, f32[32]{0:T(128)} %get-tuple-element.67, f32[32]{0:T(128)} %get-tuple-element.68, ...), kind=kLoop, calls=%fused_computation.140 | loop fusion | flops 21757952 | bytes 13897088 | tf_op jit(solution)/shard_map/convert_element_type | solution.py:150
  37.6 106.7 %all-reduce.2 = (f32[32]{0:T(128)}, f32[2,16,16]{2,1,0:T(8,128)}, f32[2,16,16]{1,2,0:T(8,128)}, f32[32]{0:T(128)}) all-reduce(f32[32]{0:T(128)} %get-tuple-element.93, f32[2,16,16]{2,1,0:T(8,128)} %fusion.215, f32[2,16,16]{1,2,0:T(8,128)} %convolution_bitcast_fusion, ...), channel_id=1, replica_groups=mesh['sample'=32,'space'=16] {'sample','space'}, use_global_device_ids=true, to_apply=%region_2.3 | all-reduce | flops 1088 | bytes 8704 | tf_op jit(solution)/shard_map/psum | solution.py:169
  158.8 1.6 fusion.212
  164.8 1.5 fusion.211
  170.3 1.5 fusion.210
  175.7 1.5 fusion.209
  194.3 1.6 fusion.208
  201.5 1.6 multiply_reduce_fusion.2
  205.8 1.5 multiply_reduce_fusion.3
  214.6 1.5 multiply_bitcast_fusion
  217.5 1.4 reshape.117
  219.0 1.7 convolution_add_fusion.1
  222.0 1.5 fusion.91
  225.0 6.7 %fusion.60 = (f32[32]{0:T(128)S(1)}, f32[32]{0:T(128)S(1)}, f32[32]{0:T(128)}, f32[32]{0:T(128)}, f32[32]{0:T(128)}, /*index=5*/f32[32]{0:T(128)}, f32[32]{0:T(1...) fusion(f32[32,4,16,128]{3,2,1,0:T(8,128)S(1)} %bitcast.164, ...), kind=kLoop, calls=%fused_computation.141 | loop fusion | flops 14155200 | bytes 10488064 | tf_op jit(solution)/shard_map/reduce_sum | solution.py:188
  235.9 4.3 fusion.57
  240.5 2.8 stack.111
  243.3 124.4 %all-reduce.3 = (f32[32,32]{1,0:T(8,128)S(1)}, f32[32,27]{0,1:T(8,128)S(1)}) all-reduce(f32[32,32]{1,0:T(8,128)} %fusion.91, f32[32,27]{0,1:T(8,128)S(1)} %stack.111), channel_id=1, replica_groups=mesh['sample'=32,'space'=16] {'sample'}, use_global_device_ids=true, to_apply=%region_11.12 | all-reduce | flops 1888 | bytes 15104 | tf_op jit(solution)/shard_map/psum | solution.py:197
  367.7 52.4 %all-reduce.4 = (f32[32,32]{1,0:T(8,128)S(1)}, f32[32,27]{0,1:T(8,128)S(1)}) all-reduce(f32[32,32]{1,0:T(8,128)S(1)} %get-tuple-element.73, f32[32,27]{0,1:T(8,128)S(1)} %get-tuple-element.74), channel_id=1, replica_groups=mesh['sample'=32,'space'=16] {'space'}, use_global_device_ids=true, to_apply=%region_12.13 | all-reduce | flops 1888 | bytes 15104 | tf_op jit(solution)/shard_map/psum | solution.py:196
  420.1 5.4 %collective-permute-start.2 = (f32[32,1,16,128]{3,2,1,0:T(8,128)}, f32[32,1,16,128]{3,2,1,0:T(8,128)S(1)}, u32[]{:S(2)}, u32[]{:S(2)}) collective-permute-start(f32[32,1,16,128]{3,2,1,0:T(8,128)} %get-tuple-element.77), channel_id=1, source_target_pairs={{0,1},{1,2},{2,3},{3,4},{4,5},{5,6},{6,7},{7,8},{8,9},{9,10},{10,1... | collective-permute-start | bytes 786440 | tf_op jit(solution)/shard_map/ppermute | solution.py:20
  425.5 1.9 collective-permute-start.3
  427.4 1.6 fusion.5
  431.2 3.9 collective-permute-done.3
  435.2 3.4 select_maximum_fusion
  438.8 25.1 %fusion.94 = bf16[1,32,4,16,128]{4,3,2,1,0:T(8,128)(2,1)} fusion(f32[32,6,18,130]{3,2,1,0:T(8,128)} %select_maximum_fusion, f32[32]{0:T(128)S(1)} %copy-done.23, f32[32]{0:T(128)S(1)} %copy-done.24, f32[32]{0:T(128)S(1)} %copy-done.26, f32[32]{0:T(128)S(1)} %copy-done.27, f32[32,4,16,128]{3,2,1,0:T(8,128)S(1)} %bitcast.168, ...), kind=kLoop, calls=%fused_computation.206 | loop fusion | flops 14680064 | bytes 27266432 | tf_op jit(solution)/shard_map/broadcast_in_dim | solution.py:203
  (181 shorter events, 78.5 us)
Async XLA Ops:
  1.8 22.1 %collective-permute-start = (bf16[32,1,16,128]{3,2,1,0:T(8,128)(2,1)S(1)}, bf16[32,1,16,128]{3,2,1,0:T(8,128)(2,1)S(1)}, u32[]{:S(2)}, u32[]{:S(2)}) collective-permute-start(bf16[32,1,16,128]{3,2,1,0:T(8,128)(2,1)S(1)} %get-tuple-element.79), channel_id=1, source_target_pairs={{0,1},{1,2},{2,3},{3,4},{4,5},{5,6},{6,7},{7,8},{8,9},{9,10},{10,1... | collective-permute-start | bytes 393224 | tf_op jit(solution)/shard_map/ppermute | solution.py:20
  6.8 17.0 %collective-permute-start.1 = (bf16[32,1,16,128]{3,2,1,0:T(8,128)(2,1)S(1)}, bf16[32,1,16,128]{3,2,1,0:T(8,128)(2,1)}, u32[]{:S(2)}, u32[]{:S(2)}) collective-permute-start(bf16[32,1,16,128]{3,2,1,0:T(8,128)(2,1)S(1)} %get-tuple-element.80), channel_id=1, source_target_pairs={{1,0},{2,1},{3,2},{4,3},{5,4},{6,5},{7,6},{8,7},{9,8},{10,9},{11,1... | collective-permute-start | bytes 393224 | tf_op jit(solution)/shard_map/ppermute | solution.py:23
  35.8 186.2 %copy-start.1 = (bf16[8192,32]{0,1:T(8,128)(2,1)}, bf16[8192,32]{0,1:T(8,128)(2,1)S(1)}, u32[]{:S(2)}) copy-start(bf16[8192,32]{0,1:T(8,128)(2,1)S(1)} %get-tuple-element.94) | copy-start | bytes 1572868
  240.3 198.2 %copy-start.17 = (f32[32]{0:T(128)S(1)}, f32[32]{0:T(128)}, u32[]{:S(2)}) copy-start(f32[32]{0:T(128)} %get-tuple-element.61) | copy-start | bytes 388
  240.3 198.2 %copy-start.18 = (f32[32]{0:T(128)S(1)}, f32[32]{0:T(128)}, u32[]{:S(2)}) copy-start(f32[32]{0:T(128)} %get-tuple-element.62) | copy-start | bytes 388
  240.3 198.2 %copy-start.19 = (f32[32]{0:T(128)S(1)}, f32[32]{0:T(128)}, u32[]{:S(2)}) copy-start(f32[32]{0:T(128)} %get-tuple-element.63) | copy-start | bytes 388
  240.3 198.2 %copy-start.20 = (f32[32]{0:T(128)S(1)}, f32[32]{0:T(128)}, u32[]{:S(2)}) copy-start(f32[32]{0:T(128)} %get-tuple-element.64) | copy-start | bytes 388
  240.3 198.3 %copy-start.21 = (f32[32]{0:T(128)S(1)}, f32[32]{0:T(128)}, u32[]{:S(2)}) copy-start(f32[32]{0:T(128)} %get-tuple-element.65) | copy-start | bytes 388
  240.3 198.3 %copy-start.22 = (f32[32]{0:T(128)S(1)}, f32[32]{0:T(128)}, u32[]{:S(2)}) copy-start(f32[32]{0:T(128)} %get-tuple-element.66) | copy-start | bytes 388
  240.3 198.3 %copy-start.23 = (f32[32]{0:T(128)S(1)}, f32[32]{0:T(128)}, u32[]{:S(2)}) copy-start(f32[32]{0:T(128)} %get-tuple-element.67) | copy-start | bytes 388
  240.3 198.3 %copy-start.24 = (f32[32]{0:T(128)S(1)}, f32[32]{0:T(128)}, u32[]{:S(2)}) copy-start(f32[32]{0:T(128)} %get-tuple-element.68) | copy-start | bytes 388
  240.3 198.3 %copy-start.25 = (f32[32]{0:T(128)S(1)}, f32[32]{0:T(128)}, u32[]{:S(2)}) copy-start(f32[32]{0:T(128)} %get-tuple-element.42) | copy-start | bytes 388
  240.3 198.3 %copy-start.26 = (f32[32]{0:T(128)S(1)}, f32[32]{0:T(128)}, u32[]{:S(2)}) copy-start(f32[32]{0:T(128)} %get-tuple-element.43) | copy-start | bytes 388
  240.3 198.3 %copy-start.27 = (f32[32]{0:T(128)S(1)}, f32[32]{0:T(128)}, u32[]{:S(2)}) copy-start(f32[32]{0:T(128)} %get-tuple-element.44) | copy-start | bytes 388
  240.4 198.3 %copy-start.28 = (f32[32]{0:T(128)S(1)}, f32[32]{0:T(128)}, u32[]{:S(2)}) copy-start(f32[32]{0:T(128)} %get-tuple-element.45) | copy-start | bytes 388
  240.4 198.3 %copy-start.29 = (f32[32]{0:T(128)S(1)}, f32[32]{0:T(128)}, u32[]{:S(2)}) copy-start(f32[32]{0:T(128)} %get-tuple-element.46) | copy-start | bytes 388
  240.4 198.3 %copy-start.30 = (f32[32]{0:T(128)S(1)}, f32[32]{0:T(128)}, u32[]{:S(2)}) copy-start(f32[32]{0:T(128)} %get-tuple-element.47) | copy-start | bytes 388
  240.4 198.3 %copy-start.31 = (f32[32]{0:T(128)S(1)}, f32[32]{0:T(128)}, u32[]{:S(2)}) copy-start(f32[32]{0:T(128)} %get-tuple-element.48) | copy-start | bytes 388
  240.4 198.3 %copy-start.32 = (f32[32]{0:T(128)S(1)}, f32[32]{0:T(128)}, u32[]{:S(2)}) copy-start(f32[32]{0:T(128)} %get-tuple-element.49) | copy-start | bytes 388
  240.4 198.3 %copy-start.33 = (f32[32]{0:T(128)S(1)}, f32[32]{0:T(128)}, u32[]{:S(2)}) copy-start(f32[32]{0:T(128)} %get-tuple-element.50) | copy-start | bytes 388
  240.4 198.3 %copy-start.34 = (f32[32]{0:T(128)S(1)}, f32[32]{0:T(128)}, u32[]{:S(2)}) copy-start(f32[32]{0:T(128)} %get-tuple-element.51) | copy-start | bytes 388
  240.4 198.3 %copy-start.35 = (f32[32]{0:T(128)S(1)}, f32[32]{0:T(128)}, u32[]{:S(2)}) copy-start(f32[32]{0:T(128)} %get-tuple-element.52) | copy-start | bytes 388
  240.4 198.3 %copy-start.36 = (f32[32]{0:T(128)S(1)}, f32[32]{0:T(128)}, u32[]{:S(2)}) copy-start(f32[32]{0:T(128)} %get-tuple-element.53) | copy-start | bytes 388
  240.4 198.3 %copy-start.37 = (f32[32]{0:T(128)S(1)}, f32[32]{0:T(128)}, u32[]{:S(2)}) copy-start(f32[32]{0:T(128)} %get-tuple-element.54) | copy-start | bytes 388
  240.5 198.3 %copy-start.38 = (f32[32]{0:T(128)S(1)}, f32[32]{0:T(128)}, u32[]{:S(2)}) copy-start(f32[32]{0:T(128)} %get-tuple-element.55) | copy-start | bytes 388
  240.5 198.3 %copy-start.39 = (f32[32]{0:T(128)S(1)}, f32[32]{0:T(128)}, u32[]{:S(2)}) copy-start(f32[32]{0:T(128)} %get-tuple-element.56) | copy-start | bytes 388
  240.5 198.3 %copy-start.40 = (f32[32]{0:T(128)S(1)}, f32[32]{0:T(128)}, u32[]{:S(2)}) copy-start(f32[32]{0:T(128)} %get-tuple-element.57) | copy-start | bytes 388
  240.5 198.3 %copy-start.41 = (f32[32]{0:T(128)S(1)}, f32[32]{0:T(128)}, u32[]{:S(2)}) copy-start(f32[32]{0:T(128)} %get-tuple-element.58) | copy-start | bytes 388
  240.5 198.3 %copy-start.42 = (f32[32]{0:T(128)S(1)}, f32[32]{0:T(128)}, u32[]{:S(2)}) copy-start(f32[32]{0:T(128)} %get-tuple-element.59) | copy-start | bytes 388
  240.5 198.3 %copy-start.43 = (f32[32]{0:T(128)S(1)}, f32[32]{0:T(128)}, u32[]{:S(2)}) copy-start(f32[32]{0:T(128)} %get-tuple-element.60) | copy-start | bytes 388
  420.1 11.1 %collective-permute-start.2 = (f32[32,1,16,128]{3,2,1,0:T(8,128)}, f32[32,1,16,128]{3,2,1,0:T(8,128)S(1)}, u32[]{:S(2)}, u32[]{:S(2)}) collective-permute-start(f32[32,1,16,128]{3,2,1,0:T(8,128)} %get-tuple-element.77), channel_id=1, source_target_pairs={{0,1},{1,2},{2,3},{3,4},{4,5},{5,6},{6,7},{7,8},{8,9},{9,10},{10,1... | collective-permute-start | bytes 786440 | tf_op jit(solution)/shard_map/ppermute | solution.py:20
  425.5 9.7 %collective-permute-start.3 = (f32[32,1,16,128]{3,2,1,0:T(8,128)}, f32[32,1,16,128]{3,2,1,0:T(8,128)S(1)}, u32[]{:S(2)}, u32[]{:S(2)}) collective-permute-start(f32[32,1,16,128]{3,2,1,0:T(8,128)} %get-tuple-element.78), channel_id=1, source_target_pairs={{1,0},{2,1},{3,2},{4,3},{5,4},{6,5},{7,6},{8,7},{9,8},{10,9},{11,1... | collective-permute-start | bytes 786440 | tf_op jit(solution)/shard_map/ppermute | solution.py:23
  (17 other events, 117.0 us)
